TPU v7x, 32 devices: a whole 2x2x4 slice. The times are simulated.
32 devices in a mesh: wide: 8 (over y, x, core), blk: 4 (over z).
Axes of the slice: x: 2, y: 2, z: 4, core: 2. Of those that a mesh axis runs over, the one named last changes fastest.
Arguments:
- audio: bfloat16 [4096, 1024], P(('wide', 'blk')), may hold values from -1 to 1
- video: bfloat16 [4096, 1024], P(('wide', 'blk')), may hold values from -1 to 1
- owner: int32 [4096, 1], P(('wide', 'blk')), may hold values from 0 to 7; in each aligned block of 128 rows (0 to 127, 128 to 255, ...) at most 32 rows name the same one
- clip_feats: bfloat16 [8192, 1024], P(('wide', 'blk')), may hold values from -24 to 24
- lengths: int32 [8192], P(('wide', 'blk')), may hold values from 1 to 16
- proj_weight: bfloat16 [1024, 1024], replicated, may hold values from -0.1875 to 0.1875
Outputs:
- audio_grad: bfloat16 [4096, 1024], P(('wide', 'blk'))
- feats_grad: bfloat16 [8192, 1024], P(('wide', 'blk'))
- weight_grad: float32 [1024, 1024], P('wide')
Inputs may be any that keep to these rules, and one draw needn't show every extreme that they name: Among the 128 rows of one device, no owner is named more than 32 times, a bound that some block reaches.
All inputs are finite; a program needn't handle non-finite values.
Results may differ from a plain program's by a relative error of at most 0.02.
Values may be sent and summed in bfloat16 or wider, within the bound.
A program may use at most 64 MiB of HBM per device.

v0:
```python
from functools import partial
import jax
import jax.numpy as jnp
from jax import lax
from jax.sharding import PartitionSpec as P


def rows_dot(matrix_a, matrix_b):
    return lax.dot_general(
        matrix_a, matrix_b, (((1,), (1,)), ((), ())), preferred_element_type=jnp.float32
    )


def cols_dot(matrix_a, matrix_b):
    return lax.dot_general(
        matrix_a, matrix_b, (((0,), (0,)), ((), ())), preferred_element_type=jnp.float32
    )


def pair_coeffs(scores, labels, factor):
    return (factor * (jax.nn.sigmoid(4.0 * scores - 2.0) - labels)).astype(jnp.bfloat16)


def shards(audio, video, owner, clip_feats, lengths, proj_weight):
    blocks = lax.axis_size("blk")
    clip_count = audio.shape[0]
    feature_count = audio.shape[1]
    factor = 4.0 / blocks
    row_ids = jnp.arange(clip_count, dtype=jnp.int32)
    offset = lax.axis_index("blk") * clip_count
    gathered = lax.all_gather(video, "blk", axis=0, tiled=True)
    other_ids = jnp.arange(gathered.shape[0], dtype=jnp.int32)
    labels = ((offset + row_ids)[:, None] == other_ids[None, :]).astype(jnp.float32)
    coeffs = pair_coeffs(rows_dot(audio, gathered), labels, factor)
    audio_total = jnp.dot(coeffs, gathered, preferred_element_type=jnp.float32)
    gathered = lax.all_gather(audio, "blk", axis=0, tiled=True)
    other_ids = jnp.arange(gathered.shape[0], dtype=jnp.int32)
    labels = (other_ids[:, None] == (offset + row_ids)[None, :]).astype(jnp.float32)
    coeffs = pair_coeffs(rows_dot(gathered, video), labels, factor)
    video_sum = cols_dot(coeffs, gathered)
    audio_grad = audio_total.astype(jnp.bfloat16)
    video_grad = video_sum.astype(jnp.bfloat16)
    peer_count = lax.axis_size("wide")
    slot_count = clip_feats.shape[0]
    capacity = slot_count // peer_count
    owner_peer = owner[:, 0]
    onehot = (owner_peer[:, None] == jnp.arange(peer_count, dtype=jnp.int32)[None, :]).astype(
        jnp.int32
    )
    slot_rank = jnp.sum((jnp.cumsum(onehot, axis=0) - onehot) * onehot, axis=1)
    target = owner_peer * capacity + slot_rank
    placing = (jnp.arange(slot_count, dtype=jnp.int32)[:, None] == target[None, :]).astype(
        jnp.bfloat16
    )
    packed = jnp.dot(placing, video_grad, preferred_element_type=jnp.float32).astype(jnp.bfloat16)
    packed = packed.reshape(peer_count, capacity, feature_count)
    received = lax.all_to_all(packed, "wide", split_axis=0, concat_axis=0, tiled=True).reshape(
        slot_count, feature_count
    )
    length_scale = lax.rsqrt(lengths.astype(jnp.float32))[:, None]
    pooled = (clip_feats.astype(jnp.float32) * length_scale).astype(jnp.bfloat16)
    preact = jnp.dot(pooled, proj_weight, preferred_element_type=jnp.float32)
    _, pullback = jax.vjp(partial(jax.nn.gelu, approximate=False), preact)
    pre_grad = pullback(received.astype(jnp.float32))[0].astype(jnp.bfloat16)
    feats_grad = (rows_dot(pre_grad, proj_weight) * length_scale).astype(jnp.bfloat16)
    partial_rows = lax.psum_scatter(
        cols_dot(pooled, pre_grad).astype(jnp.bfloat16), "wide", scatter_dimension=0, tiled=True
    )
    weight_grad = lax.psum(partial_rows, "blk").astype(jnp.float32)
    return (audio_grad, feats_grad, weight_grad)


def solution(mesh):
    return jax.shard_map(
        shards,
        mesh=mesh,
        in_specs=(
            P(("wide", "blk"), None),
            P(("wide", "blk"), None),
            P(("wide", "blk"), None),
            P(("wide", "blk"), None),
            P(("wide", "blk")),
            P(),
        ),
        out_specs=(P(("wide", "blk"), None), P(("wide", "blk"), None), P("wide", None)),
        check_vma=False,
    )
```

profile of v0, /device:TPU:0, one launch (start us, length us, event | category | flops | bytes accessed | tf_op | source)
XLA Modules:
  0.0 167.4 jit_solution(1915806834253951210)
XLA Ops:
  7.2 0.0 all-gather.5.cloned.1.call-start
  7.2 0.7 all-gather.5.cloned.1.call-update
  7.9 0.7 fusion.37
  8.7 0.2 reduce_window_sum.11
  8.8 0.8 select_reduce_fusion
  9.7 0.7 multiply_add_fusion
  10.3 30.0 %all-gather.5.cloned.1.call-done = bf16[512,1024]{1,0:T(8,128)(2,1)} async-done(((bf16[128,1024]{1,0:T(8,128)(2,1)}), bf16[512,1024]{1,0:T(8,128)(2,1)}) %all-gather.5.cloned.1.call-update) | async-done | bytes 1048592 | tf_op jit(solution)/shard_map/all_gather | solution.py:36
  40.3 1.8 %fusion.14 = bf16[512,128]{1,0:T(8,128)(2,1)S(1)} fusion(bf16[512,1024]{1,0:T(8,128)(2,1)} %all-gather.5.cloned.1.call-done, bf16[128,1024]{1,0:T(8,128)(2,1)} %param.7, s32[128]{0:T(128)S(1)} %iota_add_fusion), kind=kOutput, calls=%fused_computation.24 | convolution fusion | flops 134807552 | bytes 1442304 | tf_op jit(solution)/shard_map/dot_general | solution.py:9
  42.1 1.4 convolution_convert_fusion.1
  43.5 3.7 %all-to-all-start = ((bf16[8,32,1024]{2,1,0:T(8,128)(2,1)}), bf16[8,32,1024]{2,1,0:T(8,128)(2,1)S(1)}, u32[]{:S(2)}, u32[]{:S(2)}) async-start(bf16[8,32,1024]{2,1,0:T(8,128)(2,1)} %bitcast.1), calls=%async_computation | async-start | bytes 1048576 | tf_op jit(solution)/shard_map/all_to_all | solution.py:57
  47.2 0.0 all-gather.3.cloned.1.call-start
  47.2 0.7 all-gather.3.cloned.1.call-update
  47.9 0.0 reduce-scatter.2.cloned.1.call-start
  48.0 8.9 %all-to-all-done = bf16[8,32,1024]{2,1,0:T(8,128)(2,1)S(1)} async-done(((bf16[8,32,1024]{2,1,0:T(8,128)(2,1)}), bf16[8,32,1024]{2,1,0:T(8,128)(2,1)S(1)}, u32[]{:S(2)}, u32[]{:S(2)}) %all-to-all-start) | async-done | bytes 524320 | tf_op jit(solution)/shard_map/all_to_all | solution.py:57
  56.9 4.2 %fusion.20 = bf16[256,1024]{1,0:T(8,128)(2,1)S(1)} fusion(bf16[8,32,1024]{2,1,0:T(8,128)(2,1)S(1)} %all-to-all-done, bf16[1024,1024]{1,0:T(8,128)(2,1)S(1)} %copy-done, bf16[256,1024]{1,0:T(8,128)(2,1)} %param.9, f32[256]{0:T(256)S(1)} %convert_rsqrt_fusion), kind=kOutput, calls=%fused_computation.30 | convolution fusion | flops 556793856 | bytes 3671040 | tf_op jit(solution)/shard_map/dot_general | solution.py:62
  61.1 0.8 copy-done.3
  61.9 2.2 %convolution_convert_fusion = bf16[1024,1024]{1,0:T(8,128)(2,1)} fusion(bf16[256,1024]{1,0:T(8,128)(2,1)S(1)} %fusion.20, bf16[256,1024]{1,0:T(8,128)(2,1)S(1)} %copy-done.2, f32[256]{0:T(256)S(1)} %convert_rsqrt_fusion), kind=kOutput, calls=%fused_computation | convolution fusion | flops 538705920 | bytes 3146752 | tf_op jit(solution)/shard_map/dot_general | solution.py:15
  64.1 0.0 all-reduce.2.cloned.1.call-start
  64.2 13.3 %all-gather.3.cloned.1.call-done = bf16[512,1024]{1,0:T(8,128)(2,1)} async-done(((bf16[128,1024]{1,0:T(8,128)(2,1)}), bf16[512,1024]{1,0:T(8,128)(2,1)}) %all-gather.3.cloned.1.call-update) | async-done | bytes 1048592 | tf_op jit(solution)/shard_map/all_gather | solution.py:31
  77.5 3.1 %convolution_convert_fusion.3 = bf16[128,1024]{1,0:T(8,128)(2,1)} fusion(bf16[512,1024]{1,0:T(8,128)(2,1)} %all-gather.3.cloned.1.call-done, bf16[128,1024]{1,0:T(8,128)(2,1)S(1)} %copy-done.5, s32[128]{0:T(128)S(1)} %iota_add_fusion), kind=kOutput, calls=%fused_computation.8 | convolution fusion | flops 269156352 | bytes 1573376 | tf_op jit(solution)/shard_map/dot_general | solution.py:35
  80.5 40.8 %reduce-scatter.2.cloned.1.call-done = bf16[128,1024]{1,0:T(8,128)(2,1)} async-done(((bf16[1024,1024]{1,0:T(8,128)(2,1)}), bf16[128,1024]{1,0:T(8,128)(2,1)}) %reduce-scatter.2.cloned.1.call-update) | async-done | bytes 262160 | tf_op jit(solution)/shard_map/reduce_scatter | solution.py:66
  121.3 1.6 fusion
  122.9 36.2 %all-reduce.2.cloned.1.call-done = bf16[128,1024]{1,0:T(8,128)(2,1)} async-done(((bf16[128,1024]{1,0:T(8,128)(2,1)}), bf16[128,1024]{1,0:T(8,128)(2,1)}) %all-reduce.2.cloned.1.call-update) | async-done | bytes 262160 | tf_op jit(solution)/shard_map/psum | solution.py:69
  159.1 1.8 %convert_element_type.68 = f32[128,1024]{1,0:T(8,128)} convert(bf16[128,1024]{1,0:T(8,128)(2,1)} %all-reduce.2.cloned.1.call-done) | non-fusion elementwise | flops 131072 | bytes 786432 | tf_op jit(solution)/shard_map/convert_element_type | solution.py:69
  (17 shorter events, 0.1 us)
Async XLA Ops:
  7.2 49.7 %copy-start = (bf16[1024,1024]{1,0:T(8,128)(2,1)S(1)}, bf16[1024,1024]{1,0:T(8,128)(2,1)}, u32[]{:S(2)}) copy-start(bf16[1024,1024]{1,0:T(8,128)(2,1)} %param.11) | copy-start | bytes 6291460
  7.2 33.1 %all-gather.5.cloned.1.call-start = ((), (), s32[]{:S(2)}) async-start(), calls=%async_computation.3 | async-start | bytes 1310720 | tf_op jit(solution)/shard_map/all_gather | solution.py:36
  40.3 1.8 %copy-start.1 = (bf16[512,1024]{1,0:T(8,128)(2,1)S(1)}, bf16[512,1024]{1,0:T(8,128)(2,1)}, u32[]{:S(2)}) copy-start(bf16[512,1024]{1,0:T(8,128)(2,1)} %all-gather.5.cloned.1.call-done) | copy-start | bytes 3145732
  42.1 5.8 %copy-start.6 = (s32[256]{0:T(256)S(1)}, s32[256]{0:T(256)}, u32[]{:S(2)}) copy-start(s32[256]{0:T(256)} %param.10) | copy-start | bytes 3076
  43.5 13.4 %all-to-all-start = ((bf16[8,32,1024]{2,1,0:T(8,128)(2,1)}), bf16[8,32,1024]{2,1,0:T(8,128)(2,1)S(1)}, u32[]{:S(2)}, u32[]{:S(2)}) async-start(bf16[8,32,1024]{2,1,0:T(8,128)(2,1)} %bitcast.1), calls=%async_computation | async-start | bytes 1048576 | tf_op jit(solution)/shard_map/all_to_all | solution.py:57
  47.2 30.3 %all-gather.3.cloned.1.call-start = ((), (), s32[]{:S(2)}) async-start(), calls=%async_computation.2 | async-start | bytes 1310720 | tf_op jit(solution)/shard_map/all_gather | solution.py:31
  47.9 73.4 %reduce-scatter.2.cloned.1.call-start = ((), (), s32[]{:S(2)}) async-start(), calls=%async_computation.4 | async-start | bytes 2359296 | tf_op jit(solution)/shard_map/reduce_scatter | solution.py:66
  48.0 13.9 %copy-start.2 = (bf16[256,1024]{1,0:T(8,128)(2,1)S(1)}, bf16[256,1024]{1,0:T(8,128)(2,1)}, u32[]{:S(2)}) copy-start(bf16[256,1024]{1,0:T(8,128)(2,1)} %param.9) | copy-start | bytes 1572868
  61.1 0.8 copy-start.3
  61.9 15.6 %copy-start.5 = (bf16[128,1024]{1,0:T(8,128)(2,1)S(1)}, bf16[128,1024]{1,0:T(8,128)(2,1)}, u32[]{:S(2)}) copy-start(bf16[128,1024]{1,0:T(8,128)(2,1)} %param.6) | copy-start | bytes 786436
  64.1 57.2 %copy-start.4 = (bf16[256,1024]{1,0:T(8,128)(2,1)S(1)}, bf16[256,1024]{1,0:T(8,128)(2,1)}, u32[]{:S(2)}) copy-start(bf16[256,1024]{1,0:T(8,128)(2,1)} %copy-done.3) | copy-start | bytes 1572868
  64.1 95.0 %all-reduce.2.cloned.1.call-start = ((), (), s32[]{:S(2)}) async-start(), calls=%async_computation.5 | async-start | bytes 524288 | tf_op jit(solution)/shard_map/psum | solution.py:69
Sparse Core Ops, SparseCore 0:
  9.6 30.6 all-gather.4
  49.5 27.8 all-gather.2
  80.7 40.4 reduce-scatter.1
  123.5 35.5 all-reduce.1
where the time goes:
time: 168 us; the launch traced here: 167 us
  waiting for transfers between devices  131 us (78%)
  matrix products  14.2 us (8%)
  between operations  13.9 us (8%)
  other arithmetic  4.2 us (2%)
  starting transfers between devices  3.81 us (2%)
    reduce_scatter x1, waiting for transfers between devices, shards(): lax.psum_scatter(cols_dot(pooled, pre_grad).astype(jnp.bfloat16), 'wide',...  40.8 us
    psum x1, waiting for transfers between devices, shards(): weight_grad = lax.psum(partial_rows, 'blk').astype(jnp.float32)  36.2 us
    all_gather x1, waiting for transfers between devices, shards(): gathered = lax.all_gather(audio, 'blk', axis=0, tiled=True)  30 us
    all_gather x1, waiting for transfers between devices, shards(): gathered = lax.all_gather(video, 'blk', axis=0, tiled=True)  13.3 us
    all_to_all x1, waiting for transfers between devices, shards(): lax.all_to_all(packed, 'wide', split_axis=0, concat_axis=0, tiled=True)  8.88 us
    dot_general x1, matrix products, shards(): preact = jnp.dot(pooled, proj_weight, preferred_element_type=jnp.float32)  4.22 us
    all_to_all x1, starting transfers between devices, shards(): lax.all_to_all(packed, 'wide', split_axis=0, concat_axis=0, tiled=True)  3.65 us
    dot_general x2, matrix products, rows_dot(): lax.dot_general(matrix_a, matrix_b, (((1,), (1,)), ((), ())), preferred_e...  3.41 us
  transfers between devices with their start and end apart: 5, of which 5 were waited for; matrix products, arithmetic and copies ran while one was open for 8% of the time, Pallas kernels for 0%

commit v1 on v0

--- a/solution.py
+++ b/solution.py
@@ -33,7 +33,9 @@
     labels = ((offset + row_ids)[:, None] == other_ids[None, :]).astype(jnp.float32)
     coeffs = pair_coeffs(rows_dot(audio, gathered), labels, factor)
     audio_total = jnp.dot(coeffs, gathered, preferred_element_type=jnp.float32)
-    gathered = lax.all_gather(audio, "blk", axis=0, tiled=True)
+    gathered = jnp.concatenate(
+        lax.all_to_all(jnp.stack([audio] * lax.axis_size("blk")), "blk", 0, 0), axis=0
+    )
     other_ids = jnp.arange(gathered.shape[0], dtype=jnp.int32)
     labels = (other_ids[:, None] == (offset + row_ids)[None, :]).astype(jnp.float32)
     coeffs = pair_coeffs(rows_dot(gathered, video), labels, factor)

time: 168 us -> 149 us (0.89)
  waiting for transfers between devices: 131 us -> 104 us
  starting transfers between devices: 3.81 us -> 10.2 us
  local copies, waits for them, and re-layouts: 0.82 us -> 3.02 us
  other arithmetic: 4.2 us -> 2.23 us
  between operations: 13.9 us -> 15.6 us
    all_gather x1 -> x0, waiting for transfers between devices: 30 us -> none  [shards(): gathered = lax.all_gather(audio, 'blk', axis=0, tiled=True)]
    all_to_all x0 -> x1, waiting for transfers between devices: none -> 25.3 us  [shards(): lax.all_to_all(jnp.stack([audio] * lax.axis_size('blk')), 'blk', 0, 0)]
    reduce_scatter x1, waiting for transfers between devices: 40.8 us -> 22.3 us  [shards(): lax.psum_scatter(cols_dot(pooled, pre_grad).astype(jnp.bfloat16), 'wide',...]
    all_to_all x0 -> x1, starting transfers between devices: none -> 6.35 us  [shards(): lax.all_to_all(jnp.stack([audio] * lax.axis_size('blk')), 'blk', 0, 0)]
    another operation x0 -> x1, local copies, waits for them, and re-layouts: none -> 2.19 us  [shards(): jnp.stack([audio] * lax.axis_size('blk'))]
    psum x1, waiting for transfers between devices: 36.2 us -> 34.2 us  [shards(): weight_grad = lax.psum(partial_rows, 'blk').astype(jnp.float32)]
where the time goes in v1:
time: 149 us; the launch traced here: 148 us
  waiting for transfers between devices  104 us (70%)
  between operations  15.6 us (10%)
  matrix products  12.8 us (9%)
  starting transfers between devices  10.2 us (7%)
  local copies, waits for them, and re-layouts  3.02 us (2%)
  other arithmetic  2.23 us (1%)
    psum x1, waiting for transfers between devices, shards(): weight_grad = lax.psum(partial_rows, 'blk').astype(jnp.float32)  34.2 us
    all_to_all x1, waiting for transfers between devices, shards(): lax.all_to_all(jnp.stack([audio] * lax.axis_size('blk')), 'blk', 0, 0)  25.3 us
    reduce_scatter x1, waiting for transfers between devices, shards(): lax.psum_scatter(cols_dot(pooled, pre_grad).astype(jnp.bfloat16), 'wide',...  22.3 us
    all_gather x1, waiting for transfers between devices, shards(): gathered = lax.all_gather(video, 'blk', axis=0, tiled=True)  13 us
    all_to_all x1, waiting for transfers between devices, shards(): lax.all_to_all(packed, 'wide', split_axis=0, concat_axis=0, tiled=True)  8.89 us
    all_to_all x1, starting transfers between devices, shards(): lax.all_to_all(jnp.stack([audio] * lax.axis_size('blk')), 'blk', 0, 0)  6.35 us
    dot_general x1, matrix products, shards(): preact = jnp.dot(pooled, proj_weight, preferred_element_type=jnp.float32)  4.22 us
    all_to_all x1, starting transfers between devices, shards(): lax.all_to_all(packed, 'wide', split_axis=0, concat_axis=0, tiled=True)  3.72 us
  transfers between devices with their start and end apart: 5, of which 5 were waited for; matrix products, arithmetic and copies ran while one was open for 8% of the time, Pallas kernels for 0%

profile of v1, /device:TPU:0, one launch (start us, length us, event | category | flops | bytes accessed | tf_op | source)
XLA Modules:
  0.0 148.1 jit_solution(2604914790261383413)
XLA Ops:
  8.0 2.2 %stack.2 = bf16[4,128,1024]{2,1,0:T(8,128)(2,1)} broadcast(bf16[128,1024]{1,0:T(8,128)(2,1)} %param.6), dimensions={1,2} | broadcast | bytes 1310720 | tf_op jit(solution)/shard_map/stack | solution.py:37
  10.2 6.3 %all-to-all-start = ((bf16[4,128,1024]{2,1,0:T(8,128)(2,1)}), bf16[4,128,1024]{2,1,0:T(8,128)(2,1)S(1)}, u32[]{:S(2)}, u32[]{:S(2)}) async-start(bf16[4,128,1024]{2,1,0:T(8,128)(2,1)} %stack.2), calls=%async_computation | async-start | bytes 2097152 | tf_op jit(solution)/shard_map/all_to_all | solution.py:37
  16.6 0.1 fusion.37
  16.7 0.2 reduce_window_sum.11
  16.8 0.2 select_reduce_fusion
  17.0 25.3 %all-to-all-done = bf16[4,128,1024]{2,1,0:T(8,128)(2,1)S(1)} async-done(((bf16[4,128,1024]{2,1,0:T(8,128)(2,1)}), bf16[4,128,1024]{2,1,0:T(8,128)(2,1)S(1)}, u32[]{:S(2)}, u32[]{:S(2)}) %all-to-all-start) | async-done | bytes 1048608 | tf_op jit(solution)/shard_map/all_to_all | solution.py:37
  42.3 0.5 fusion.14
  42.8 1.4 convolution_convert_fusion.1
  44.1 3.7 %all-to-all-start.1 = ((bf16[8,32,1024]{2,1,0:T(8,128)(2,1)}), bf16[8,32,1024]{2,1,0:T(8,128)(2,1)S(1)}, u32[]{:S(2)}, u32[]{:S(2)}) async-start(bf16[8,32,1024]{2,1,0:T(8,128)(2,1)} %bitcast.20), calls=%async_computation.1 | async-start | bytes 1048576 | tf_op jit(solution)/shard_map/all_to_all | solution.py:59
  47.9 0.0 all-gather.2.cloned.1.call-start
  47.9 0.7 all-gather.2.cloned.1.call-update
  48.6 0.0 reduce-scatter.2.cloned.1.call-start
  48.7 8.9 %all-to-all-done.1 = bf16[8,32,1024]{2,1,0:T(8,128)(2,1)S(1)} async-done(((bf16[8,32,1024]{2,1,0:T(8,128)(2,1)}), bf16[8,32,1024]{2,1,0:T(8,128)(2,1)S(1)}, u32[]{:S(2)}, u32[]{:S(2)}) %all-to-all-start.1) | async-done | bytes 524320 | tf_op jit(solution)/shard_map/all_to_all | solution.py:59
  57.6 4.2 %fusion.20 = bf16[256,1024]{1,0:T(8,128)(2,1)S(1)} fusion(bf16[8,32,1024]{2,1,0:T(8,128)(2,1)S(1)} %all-to-all-done.1, bf16[1024,1024]{1,0:T(8,128)(2,1)S(1)} %copy-done, bf16[256,1024]{1,0:T(8,128)(2,1)} %param.9, f32[256]{0:T(256)S(1)} %convert_rsqrt_fusion), kind=kOutput, calls=%fused_computation.30 | convolution fusion | flops 556793856 | bytes 3671040 | tf_op jit(solution)/shard_map/dot_general | solution.py:64
  61.8 0.8 copy-done.2
  62.6 2.2 %convolution_convert_fusion = bf16[1024,1024]{1,0:T(8,128)(2,1)} fusion(bf16[256,1024]{1,0:T(8,128)(2,1)S(1)} %fusion.20, bf16[256,1024]{1,0:T(8,128)(2,1)S(1)} %copy-done.1, f32[256]{0:T(256)S(1)} %convert_rsqrt_fusion), kind=kOutput, calls=%fused_computation | convolution fusion | flops 538705920 | bytes 3146752 | tf_op jit(solution)/shard_map/dot_general | solution.py:15
  64.8 0.0 reduce-scatter.2.cloned.1.call-update
  64.8 0.0 all-reduce.2.cloned.1.call-start
  64.9 13.0 %all-gather.2.cloned.1.call-done = bf16[512,1024]{1,0:T(8,128)(2,1)} async-done(((bf16[128,1024]{1,0:T(8,128)(2,1)}), bf16[512,1024]{1,0:T(8,128)(2,1)}) %all-gather.2.cloned.1.call-update) | async-done | bytes 1048592 | tf_op jit(solution)/shard_map/all_gather | solution.py:31
  77.8 3.0 %convolution_convert_fusion.3 = bf16[128,1024]{1,0:T(8,128)(2,1)} fusion(bf16[512,1024]{1,0:T(8,128)(2,1)} %all-gather.2.cloned.1.call-done, bf16[128,1024]{1,0:T(8,128)(2,1)S(1)} %copy-done.4, s32[128]{0:T(128)S(1)} %iota_add_fusion), kind=kOutput, calls=%fused_computation.8 | convolution fusion | flops 269156352 | bytes 1573376 | tf_op jit(solution)/shard_map/dot_general | solution.py:35
  80.9 22.3 %reduce-scatter.2.cloned.1.call-done = bf16[128,1024]{1,0:T(8,128)(2,1)} async-done(((bf16[1024,1024]{1,0:T(8,128)(2,1)}), bf16[128,1024]{1,0:T(8,128)(2,1)}) %reduce-scatter.2.cloned.1.call-update) | async-done | bytes 262160 | tf_op jit(solution)/shard_map/reduce_scatter | solution.py:68
  103.2 1.5 %fusion = bf16[256,1024]{1,0:T(8,128)(2,1)} fusion(bf16[256,1024]{1,0:T(8,128)(2,1)S(1)} %copy-done.3, bf16[1024,1024]{1,0:T(8,128)(2,1)S(1)} %copy-done, f32[256]{0:T(256)S(1)} %convert_rsqrt_fusion), kind=kOutput, calls=%fused_computation.5 | convolution fusion | flops 537395200 | bytes 3146752 | tf_op jit(solution)/shard_map/dot_general | solution.py:9
  104.7 34.2 %all-reduce.2.cloned.1.call-done = bf16[128,1024]{1,0:T(8,128)(2,1)} async-done(((bf16[128,1024]{1,0:T(8,128)(2,1)}), bf16[128,1024]{1,0:T(8,128)(2,1)}) %all-reduce.2.cloned.1.call-update) | async-done | bytes 262160 | tf_op jit(solution)/shard_map/psum | solution.py:71
  138.9 1.8 %convert_element_type.68 = f32[128,1024]{1,0:T(8,128)} convert(bf16[128,1024]{1,0:T(8,128)(2,1)} %all-reduce.2.cloned.1.call-done) | non-fusion elementwise | flops 131072 | bytes 786432 | tf_op jit(solution)/shard_map/convert_element_type | solution.py:71
  (19 shorter events, 0.1 us)
Async XLA Ops:
  8.0 49.6 %copy-start = (bf16[1024,1024]{1,0:T(8,128)(2,1)S(1)}, bf16[1024,1024]{1,0:T(8,128)(2,1)}, u32[]{:S(2)}) copy-start(bf16[1024,1024]{1,0:T(8,128)(2,1)} %param.11) | copy-start | bytes 6291460
  8.0 8.6 %copy-start.6 = (s32[128,1]{0,1:T(1,128)S(1)}, s32[128,1]{0,1:T(1,128)}, u32[]{:S(2)}) copy-start(s32[128,1]{0,1:T(1,128)} %param.8) | copy-start | bytes 1540
  8.0 34.3 %copy-start.5 = (bf16[128,1024]{1,0:T(8,128)(2,1)S(1)}, bf16[128,1024]{1,0:T(8,128)(2,1)}, u32[]{:S(2)}) copy-start(bf16[128,1024]{1,0:T(8,128)(2,1)} %param.7) | copy-start | bytes 786436
  10.2 32.1 %all-to-all-start = ((bf16[4,128,1024]{2,1,0:T(8,128)(2,1)}), bf16[4,128,1024]{2,1,0:T(8,128)(2,1)S(1)}, u32[]{:S(2)}, u32[]{:S(2)}) async-start(bf16[4,128,1024]{2,1,0:T(8,128)(2,1)} %stack.2), calls=%async_computation | async-start | bytes 2097152 | tf_op jit(solution)/shard_map/all_to_all | solution.py:37
  42.8 5.9 %copy-start.7 = (s32[256]{0:T(256)S(1)}, s32[256]{0:T(256)}, u32[]{:S(2)}) copy-start(s32[256]{0:T(256)} %param.10) | copy-start | bytes 3076
  44.1 13.4 %all-to-all-start.1 = ((bf16[8,32,1024]{2,1,0:T(8,128)(2,1)}), bf16[8,32,1024]{2,1,0:T(8,128)(2,1)S(1)}, u32[]{:S(2)}, u32[]{:S(2)}) async-start(bf16[8,32,1024]{2,1,0:T(8,128)(2,1)} %bitcast.20), calls=%async_computation.1 | async-start | bytes 1048576 | tf_op jit(solution)/shard_map/all_to_all | solution.py:59
  47.9 30.0 %all-gather.2.cloned.1.call-start = ((), (), s32[]{:S(2)}) async-start(), calls=%async_computation.3 | async-start | bytes 1310720 | tf_op jit(solution)/shard_map/all_gather | solution.py:31
  48.6 54.5 %reduce-scatter.2.cloned.1.call-start = ((), (), s32[]{:S(2)}) async-start(), calls=%async_computation.4 | async-start | bytes 2359296 | tf_op jit(solution)/shard_map/reduce_scatter | solution.py:68
  48.7 13.9 %copy-start.1 = (bf16[256,1024]{1,0:T(8,128)(2,1)S(1)}, bf16[256,1024]{1,0:T(8,128)(2,1)}, u32[]{:S(2)}) copy-start(bf16[256,1024]{1,0:T(8,128)(2,1)} %param.9) | copy-start | bytes 1572868
  61.8 0.8 copy-start.2
  62.6 15.2 %copy-start.4 = (bf16[128,1024]{1,0:T(8,128)(2,1)S(1)}, bf16[128,1024]{1,0:T(8,128)(2,1)}, u32[]{:S(2)}) copy-start(bf16[128,1024]{1,0:T(8,128)(2,1)} %param.6) | copy-start | bytes 786436
  64.8 38.4 %copy-start.3 = (bf16[256,1024]{1,0:T(8,128)(2,1)S(1)}, bf16[256,1024]{1,0:T(8,128)(2,1)}, u32[]{:S(2)}) copy-start(bf16[256,1024]{1,0:T(8,128)(2,1)} %copy-done.2) | copy-start | bytes 1572868
  64.8 74.0 %all-reduce.2.cloned.1.call-start = ((), (), s32[]{:S(2)}) async-start(), calls=%async_computation.5 | async-start | bytes 524288 | tf_op jit(solution)/shard_map/psum | solution.py:71
Sparse Core Ops, SparseCore 0:
  50.2 27.5 all-gather.1
  103.3 35.5 all-reduce.1
Sparse Core Ops, SparseCore 1:
  64.9 38.2 reduce-scatter.1
